TPU v7x, 256 devices: a whole 4x4x8 slice. The times are simulated.
256 devices in a mesh: band: 32 (over y_hi, z, core), fft: 8 (over y_lo, x).
Axes of the slice: x: 4, y: 4 (y_hi: 2, y_lo: 2; y = y_hi * 2 + y_lo), z: 8, core: 2. Of those that a mesh axis runs over, the one named last changes fastest.
Arguments:
- orbitals: float32 [64, 96, 9216], P('band', 'fft'), may hold values from -6 to 6
- owners: int32 [1], replicated, may hold values from 0 to 31
- cutoff_mask: int32 [96, 9216], P(None, 'fft'), may hold values from 0 to 1, as said below
Outputs:
- exchange_local: float32 [64, 96, 9216], P('band', 'fft')
- exchange_block: float32 [2, 96, 9216], P(None, 'fft')
Inputs may be any that keep to these rules, and one draw needn't show every extreme that they name: cutoff_mask is 1 exactly at the frequencies whose squared length s(x)^2 + s(y)^2 + s(z)^2 lies between 1 and a cutoff, and 0 elsewhere (0 at frequency (0, 0, 0)); it is unchanged when the sign of any one frequency component is changed.
All inputs are finite; a program needn't handle non-finite values.
Results may differ from a plain program's by a relative error of at most 0.00029.
Values sent between devices are 32-bit elements; how exact they have to be, the bound alone decides.
A program may use at most 128 MiB of HBM per device.

v0:
```python
import math
import jax
import jax.numpy as jnp
from jax import lax
from jax.sharding import PartitionSpec as P

COULOMB = 400.0
EXCHANGE_MIX = 0.25


def broadcast(value, axis, source):
    kept = jnp.where(lax.axis_index(axis) == source, value, 0).astype(value.dtype)
    return lax.psum(kept, axis)


def dft_tables(count):
    positions = jnp.arange(count, dtype=jnp.int32)
    phases = positions[:, None] * positions[None, :] % count
    angles = phases.astype(jnp.float32) * (2.0 * math.pi / count)
    return (jnp.cos(angles), jnp.sin(angles))


def transform_dim(values, matrix, dim):
    source = "pabc"
    target = source[:dim] + "k" + source[dim + 1 :]
    pattern = source + "," + source[dim] + "k" + "->" + target
    return jnp.einsum(pattern, values, matrix, precision=lax.Precision.HIGHEST)


def forward_local(real_data, cosine, sine):
    casine = cosine + sine
    parts = [transform_dim(transform_dim(real_data, casine, 3), casine, 2)]
    stacked = jnp.stack(parts, axis=1)
    return stacked.reshape(stacked.shape[0], stacked.shape[1], stacked.shape[2], -1)


def spectral_middle(spectrum, kernel, cosine, sine):
    count_pairs, components, grid_size, flat_cells = spectrum.shape
    shaped = spectrum.reshape(count_pairs, components, grid_size, kernel.shape[1], grid_size)
    casine = cosine + sine
    scaled = transform_dim(shaped[:, 0], casine, 1) * kernel
    parts = [transform_dim(scaled, casine, 1)]
    return jnp.stack(parts, axis=1).reshape(count_pairs, components, grid_size, flat_cells)


def inverse_local(spectrum, cosine, sine):
    count_pairs, components, slab_rows, flat_cells = spectrum.shape
    grid_size = cosine.shape[0]
    shaped = spectrum.reshape(count_pairs, components, slab_rows, grid_size, grid_size)
    casine = cosine + sine
    result = transform_dim(transform_dim(shaped[:, 0], casine, 2), casine, 3)
    result = result / float(grid_size * grid_size * grid_size)
    return result.reshape(count_pairs, slab_rows, flat_cells)


def per_device(orbitals, owners, cutoff_mask):
    local_bands, slab_rows, flat_cells = orbitals.shape
    grid_size = slab_rows * lax.axis_size("fft")
    cosine, sine = dft_tables(grid_size)
    positions = jnp.arange(grid_size, dtype=jnp.int32)
    signed = jnp.where(positions <= grid_size // 2, positions, positions - grid_size)
    signed_y = lax.dynamic_slice_in_dim(signed, lax.axis_index("fft") * slab_rows, slab_rows)
    squared = (
        signed[:, None, None] * signed[:, None, None]
        + signed_y[None, :, None] * signed_y[None, :, None]
        + signed[None, None, :] * signed[None, None, :]
    )
    weights = cutoff_mask.reshape(grid_size, slab_rows, grid_size).astype(jnp.float32)
    kernel = COULOMB * weights / jnp.maximum(squared, 1).astype(jnp.float32)
    local_total = jnp.zeros((local_bands, slab_rows, flat_cells), jnp.float32)
    block_orbs = broadcast(orbitals, "band", owners[0])
    pair_data = (orbitals[:, None] * block_orbs[None]).reshape(
        local_bands * local_bands, slab_rows, grid_size, grid_size
    )
    spectrum = forward_local(pair_data, cosine, sine)

    def one_pair(single):
        sent = lax.all_to_all(single[None], "fft", split_axis=3, concat_axis=2, tiled=True)
        pencil_out = spectral_middle(sent, kernel, cosine, sine)
        return lax.all_to_all(pencil_out, "fft", split_axis=2, concat_axis=3, tiled=True)[0]

    returned = lax.map(one_pair, spectrum)
    potential = inverse_local(returned, cosine, sine).reshape(
        local_bands, local_bands, slab_rows, flat_cells
    )
    local_total = local_total - EXCHANGE_MIX * jnp.sum(block_orbs[None] * potential, axis=1)
    block_terms = -EXCHANGE_MIX * jnp.sum(orbitals[:, None] * potential, axis=0)
    block_total = lax.psum(block_terms, "band")
    return (local_total, block_total)


def solution(mesh):
    in_specs = (P("band", "fft", None), P(), P(None, "fft"))
    out_specs = (P("band", "fft", None), P(None, "fft", None))
    return jax.shard_map(
        per_device, mesh=mesh, in_specs=in_specs, out_specs=out_specs, check_vma=False
    )
```

profile of v0, /device:TPU:1, one launch (start us, length us, event | category | flops | bytes accessed | tf_op | source)
XLA Modules:
  0.0 1006.4 jit_solution(8958187725105323984)
XLA Ops:
  10.0 267.7 %all-reduce.3.cloned.1.call-done = f32[2,12,9216]{2,0,1:T(2,128)} async-done(((f32[2,12,9216]{2,0,1:T(2,128)}), f32[2,12,9216]{2,0,1:T(2,128)}) %all-reduce.3.cloned.1.call-update) | async-done | bytes 884752 | tf_op jit(solution)/shard_map/psum | solution.py:13
  292.4 12.8 %copy.59 = f32[4,12,96,96]{1,0,3,2:T(4,128)} copy(f32[4,12,96,96]{3,2,1,0:T(8,128)} %convolution_bitcast_fusion.1) | data formatting | bytes 3538944
  305.2 395.2 %while.14 = (s32[]{:T(128)}, f32[4,1,12,9216]{3,1,2,0:T(1,128)}, f32[4,1,12,9216]{2,1,0,3:T(1,128)}, f32[96,12,96]{0,2,1:T(8,128)S(1)}, s32[]{:T(128)}, /*index=5*/f32[]{:T(128)}, f32[]{:T(128)}) while((s32[]{:T(128)}, f32[4,1,12,9216]{3,1,2,0:T(1,128)}, f32[4,1,12,9216]{2,1,0,3:T(1,128)}, f32[96,12,96]{0,2,1:T(8,128)S(1)}, ...), condition=%wide.region_2.3_spmd.clone.clone, body=%wide.region_1.2_spmd.clone.clone.sunk | while | flops 255098880 | bytes 14155925 | solution.py:82
  322.9 43.0 %reduce.5 = f32[9216,12]{1,0:T(8,128)} reduce(f32[9216,1,1,12]{3,2,1,0:T(1,128)} %fusion.62, f32[]{:T(128)} %broadcast.59), dimensions={1,2}, to_apply=%fusion.51.reduce_sub_computation | reduce | bytes 884740 | tf_op jit(solution)/shard_map/while
  371.9 11.1 %all_to_all.58 = f32[8,1,13824]{2,1,0:T(1,128)S(1)} all-to-all(f32[8,1,13824]{2,1,0:T(1,128)S(1)} %reshape.105), channel_id=1, replica_groups=mesh['band'=32,'fft'=8] {'fft'}, dimensions={0} | all-to-all | bytes 884736 | tf_op jit(solution)/shard_map/while/body/eval_jaxpr/all_to_all | solution.py:78
  385.2 10.4 %reshape.106 = f32[9216,1,1,12]{3,2,1,0:T(1,128)} reshape(f32[8,13824]{1,0:T(8,128)S(1)} %reduce.6) | data formatting | bytes 884736 | tf_op jit(solution)/shard_map/while
  406.5 7.0 all-to-all-done.1
  419.8 43.0 %reduce.5 = f32[9216,12]{1,0:T(8,128)} reduce(f32[9216,1,1,12]{3,2,1,0:T(1,128)} %fusion.62, f32[]{:T(128)} %broadcast.59), dimensions={1,2}, to_apply=%fusion.51.reduce_sub_computation | reduce | bytes 884740 | tf_op jit(solution)/shard_map/while
  462.8 6.0 reshape.105
  468.8 9.6 all_to_all.58
  480.6 10.4 %reshape.106 = f32[9216,1,1,12]{3,2,1,0:T(1,128)} reshape(f32[8,13824]{1,0:T(8,128)S(1)} %reduce.6) | data formatting | bytes 884736 | tf_op jit(solution)/shard_map/while
  501.9 7.0 all-to-all-done.1
  515.2 43.0 %reduce.5 = f32[9216,12]{1,0:T(8,128)} reduce(f32[9216,1,1,12]{3,2,1,0:T(1,128)} %fusion.62, f32[]{:T(128)} %broadcast.59), dimensions={1,2}, to_apply=%fusion.51.reduce_sub_computation | reduce | bytes 884740 | tf_op jit(solution)/shard_map/while
  558.2 6.0 reshape.105
  564.2 9.5 all_to_all.58
  575.9 10.4 %reshape.106 = f32[9216,1,1,12]{3,2,1,0:T(1,128)} reshape(f32[8,13824]{1,0:T(8,128)S(1)} %reduce.6) | data formatting | bytes 884736 | tf_op jit(solution)/shard_map/while
  597.2 7.0 all-to-all-done.1
  610.5 43.0 %reduce.5 = f32[9216,12]{1,0:T(8,128)} reduce(f32[9216,1,1,12]{3,2,1,0:T(1,128)} %fusion.62, f32[]{:T(128)} %broadcast.59), dimensions={1,2}, to_apply=%fusion.51.reduce_sub_computation | reduce | bytes 884740 | tf_op jit(solution)/shard_map/while
  653.5 6.0 reshape.105
  659.5 9.5 all_to_all.58
  671.2 10.4 %reshape.106 = f32[9216,1,1,12]{3,2,1,0:T(1,128)} reshape(f32[8,13824]{1,0:T(8,128)S(1)} %reduce.6) | data formatting | bytes 884736 | tf_op jit(solution)/shard_map/while
  692.5 7.0 all-to-all-done.1
  716.9 8.7 multiply_reduce_fusion
  728.3 268.7 %all-reduce.5.cloned.1.call-done = f32[2,12,9216]{2,0,1:T(2,128)} async-done(((f32[2,12,9216]{2,0,1:T(2,128)}), f32[2,12,9216]{2,0,1:T(2,128)}) %all-reduce.5.cloned.1.call-update) | async-done | bytes 884752 | tf_op jit(solution)/shard_map/psum | solution.py:88
  (82 shorter events, 121.3 us)
Async XLA Ops:
  7.2 2.1 copy-start.1
  7.2 270.5 %all-reduce.3.cloned.1.call-start = ((), (), s32[]{:S(2)}) async-start(), calls=%async_computation.2 | async-start | bytes 1769472 | tf_op jit(solution)/shard_map/psum | solution.py:13
  9.2 268.4 %copy-start = (f32[2,12,9216]{2,0,1:T(2,128)S(1)}, f32[2,12,9216]{2,0,1:T(2,128)}, u32[]{:S(2)}) copy-start(f32[2,12,9216]{2,0,1:T(2,128)} %param.5) | copy-start | bytes 2654212
  9.2 987.7 %all-reduce.5.cloned.1.call-start = ((), (), s32[]{:S(2)}) async-start(), calls=%async_computation.3 | async-start | bytes 1769472 | tf_op jit(solution)/shard_map/psum | solution.py:88
  403.0 10.5 %all-to-all-start.1 = ((f32[1,1,96,1152]{3,1,0,2:T(1,128)}), f32[1,1,96,1152]{3,1,0,2:T(1,128)S(1)}, u32[]{:S(2)}, u32[]{:S(2)}) async-start(f32[1,1,96,1152]{3,1,0,2:T(1,128)} %copy.75), calls=%async_computation.1 | async-start | bytes 884736 | tf_op jit(solution)/shard_map/while/body/eval_jaxpr/all_to_all | solution.py:80
  498.4 10.5 %all-to-all-start.1 = ((f32[1,1,96,1152]{3,1,0,2:T(1,128)}), f32[1,1,96,1152]{3,1,0,2:T(1,128)S(1)}, u32[]{:S(2)}, u32[]{:S(2)}) async-start(f32[1,1,96,1152]{3,1,0,2:T(1,128)} %copy.75), calls=%async_computation.1 | async-start | bytes 884736 | tf_op jit(solution)/shard_map/while/body/eval_jaxpr/all_to_all | solution.py:80
  593.7 10.5 %all-to-all-start.1 = ((f32[1,1,96,1152]{3,1,0,2:T(1,128)}), f32[1,1,96,1152]{3,1,0,2:T(1,128)S(1)}, u32[]{:S(2)}, u32[]{:S(2)}) async-start(f32[1,1,96,1152]{3,1,0,2:T(1,128)} %copy.75), calls=%async_computation.1 | async-start | bytes 884736 | tf_op jit(solution)/shard_map/while/body/eval_jaxpr/all_to_all | solution.py:80
  689.0 10.5 %all-to-all-start.1 = ((f32[1,1,96,1152]{3,1,0,2:T(1,128)}), f32[1,1,96,1152]{3,1,0,2:T(1,128)S(1)}, u32[]{:S(2)}, u32[]{:S(2)}) async-start(f32[1,1,96,1152]{3,1,0,2:T(1,128)} %copy.75), calls=%async_computation.1 | async-start | bytes 884736 | tf_op jit(solution)/shard_map/while/body/eval_jaxpr/all_to_all | solution.py:80
Sparse Core Ops, SparseCore 0:
  11.2 266.4 all-reduce.2
  727.0 269.8 all-reduce.4
where the time goes:
time: 1010 us
  waiting for transfers between devices  565 us (56%)
  other arithmetic  201 us (20%)
  local copies, waits for them, and re-layouts  136 us (13%)
  blocking collectives  39.7 us (4%)
  matrix products  23.2 us (2%)
  between operations  15.3 us (2%)
  starting transfers between devices  14 us (1%)
  loops' own time  12.6 us (1%)
    psum x1, waiting for transfers between devices, per_device(): block_total = lax.psum(block_terms, 'band')  269 us
    psum x1, waiting for transfers between devices, broadcast(): return lax.psum(kept, axis)  268 us
    while x4, other arithmetic  172 us
    while x16, local copies, waits for them, and re-layouts  86.9 us
    all_to_all x4, blocking collectives, one_pair(): lax.all_to_all(single[None], 'fft', split_axis=3, concat_axis=2, tiled=True)  39.7 us
    all_to_all x4, waiting for transfers between devices, one_pair(): lax.all_to_all(pencil_out, 'fft', split_axis=2, concat_axis=3, tiled=True)  28.1 us
    dot_general x12, matrix products, transform_dim(): return jnp.einsum(pattern, values, matrix, precision=lax.Precision.HIGHEST)  23.2 us
  transfers between devices with their start and end apart: 6, of which 6 were waited for; matrix products, arithmetic and copies ran while one was open for 0% of the time, Pallas kernels for 0%

commit v1 on v0

--- a/solution.py
+++ b/solution.py
@@ -75,7 +75,12 @@
     spectrum = forward_local(pair_data, cosine, sine)
 
     def one_pair(single):
-        sent = lax.all_to_all(single[None], "fft", split_axis=3, concat_axis=2, tiled=True)
+        sent = jnp.concatenate(
+            lax.all_to_all(
+                jnp.stack(jnp.split(single[None], lax.axis_size("fft"), axis=3)), "fft", 0, 0
+            ),
+            axis=2,
+        )
         pencil_out = spectral_middle(sent, kernel, cosine, sine)
         return lax.all_to_all(pencil_out, "fft", split_axis=2, concat_axis=3, tiled=True)[0]
 

time: 1010 us -> 743 us (0.74)
  other arithmetic: 201 us -> 26 us
  local copies, waits for them, and re-layouts: 136 us -> 62 us
  loops' own time: 12.6 us -> 0.21 us
    while x4 -> x0, other arithmetic: 172 us -> none
    while x16 -> x28, local copies, waits for them, and re-layouts: 86.9 us -> 31.3 us
    all_to_all x12 -> x0, local copies, waits for them, and re-layouts: 15.9 us -> none  [one_pair(): lax.all_to_all(single[None], 'fft', split_axis=3, concat_axis=2, tiled=True)]
    unnamed x6 -> x7, local copies, waits for them, and re-layouts: 15 us -> 2.15 us
    another operation x1, loops' own time: 12.6 us -> 0.21 us  [per_device(): returned = lax.map(one_pair, spectrum)]
    another operation x4 -> x10, local copies, waits for them, and re-layouts: 1.72 us -> 12.7 us  [the longest x2 6.46 us: forward_local(): stacked.reshape(stacked.shape[0], stacked.shape[1], stacked.shape[2], -1)]
where the time goes in v1:
time: 743 us; the launch traced here: 741 us
  waiting for transfers between devices  565 us (76%)
  local copies, waits for them, and re-layouts  62 us (8%)
  blocking collectives  39.7 us (5%)
  other arithmetic  26 us (3%)
  matrix products  20.2 us (3%)
  between operations  14.9 us (2%)
  starting transfers between devices  14 us (2%)
    psum x1, waiting for transfers between devices, per_device(): block_total = lax.psum(block_terms, 'band')  269 us
    psum x1, waiting for transfers between devices, broadcast(): return lax.psum(kept, axis)  268 us
    all_to_all x4, blocking collectives, one_pair(): lax.all_to_all(jnp.stack(jnp.split(single[None], lax.axis_size('fft'), ax...  39.7 us
    while x28, local copies, waits for them, and re-layouts  31.3 us
    all_to_all x4, waiting for transfers between devices, one_pair(): lax.all_to_all(pencil_out, 'fft', split_axis=2, concat_axis=3, tiled=True)  28.1 us
    dot_general x12, matrix products, transform_dim(): return jnp.einsum(pattern, values, matrix, precision=lax.Precision.HIGHEST)  20.2 us
  transfers between devices with their start and end apart: 6, of which 6 were waited for; matrix products, arithmetic and copies ran while one was open for 0% of the time, Pallas kernels for 0%

profile of v1, /device:TPU:1, one launch (start us, length us, event | category | flops | bytes accessed | tf_op | source)
XLA Modules:
  0.0 741.3 jit_solution(6524608287483820901)
XLA Ops:
  10.0 267.7 %all-reduce.3.cloned.1.call-done = f32[2,12,9216]{2,0,1:T(2,128)} async-done(((f32[2,12,9216]{2,0,1:T(2,128)}), f32[2,12,9216]{2,0,1:T(2,128)}) %all-reduce.3.cloned.1.call-update) | async-done | bytes 884752 | tf_op jit(solution)/shard_map/psum | solution.py:13
  277.6 3.3 broadcast_multiply_fusion
  280.9 2.7 mul.147
  285.9 2.4 convolution_bitcast_fusion.1
  288.3 2.5 reshape.95
  290.8 4.0 copy.43
  294.8 141.3 %while.14 = (s32[]{:T(128)}, f32[4,1,12,9216]{3,1,2,0:T(1,128)}, f32[4,1,12,9216]{3,0,2,1:T(4,128)}, f32[96,12,96]{0,2,1:T(8,128)S(1)}, s32[]{:T(128)}, /*index=...) while((s32[]{:T(128)}, f32[4,1,12,9216]{3,1,2,0:T(1,128)}, ...), condition=%wide.region_2.3_spmd.clone.clone, body=%wide.region_1.2_spmd.clone.clone.sunk | while | flops 255098880 | bytes 9732421 | solution.py:87
  303.8 11.1 %all_to_all.42 = f32[8,1,1,12,1152]{4,2,3,1,0:T(1,128)S(1)} all-to-all(f32[8,1,1,12,1152]{4,2,3,1,0:T(1,128)S(1)} %fusion.83), channel_id=1, replica_groups=mesh['band'=32,'fft'=8] {'fft'}, dimensions={0} | all-to-all | bytes 884736 | tf_op jit(solution)/shard_map/while/body/eval_jaxpr/all_to_all | solution.py:79
  319.9 3.5 all-to-all-start.1
  323.3 7.0 all-to-all-done.1
  340.2 9.6 %all_to_all.42 = f32[8,1,1,12,1152]{4,2,3,1,0:T(1,128)S(1)} all-to-all(f32[8,1,1,12,1152]{4,2,3,1,0:T(1,128)S(1)} %fusion.83), channel_id=1, replica_groups=mesh['band'=32,'fft'=8] {'fft'}, dimensions={0} | all-to-all | bytes 884736 | tf_op jit(solution)/shard_map/while/body/eval_jaxpr/all_to_all | solution.py:79
  354.9 3.5 all-to-all-start.1
  358.4 7.0 all-to-all-done.1
  375.3 9.5 %all_to_all.42 = f32[8,1,1,12,1152]{4,2,3,1,0:T(1,128)S(1)} all-to-all(f32[8,1,1,12,1152]{4,2,3,1,0:T(1,128)S(1)} %fusion.83), channel_id=1, replica_groups=mesh['band'=32,'fft'=8] {'fft'}, dimensions={0} | all-to-all | bytes 884736 | tf_op jit(solution)/shard_map/while/body/eval_jaxpr/all_to_all | solution.py:79
  389.8 3.5 all-to-all-start.1
  393.3 7.0 all-to-all-done.1
  410.1 9.5 %all_to_all.42 = f32[8,1,1,12,1152]{4,2,3,1,0:T(1,128)S(1)} all-to-all(f32[8,1,1,12,1152]{4,2,3,1,0:T(1,128)S(1)} %fusion.83), channel_id=1, replica_groups=mesh['band'=32,'fft'=8] {'fft'}, dimensions={0} | all-to-all | bytes 884736 | tf_op jit(solution)/shard_map/while/body/eval_jaxpr/all_to_all | solution.py:79
  424.7 3.5 all-to-all-start.1
  428.2 7.0 all-to-all-done.1
  436.1 5.7 reduce.1
  443.8 4.0 fusion.41
  450.1 2.5 reshape.97
  452.6 8.4 %multiply_reduce_fusion = (f32[2,12,9216]{2,0,1:T(2,128)S(1)}, f32[2,12,9216]{2,0,1:T(2,128)S(1)}) fusion(f32[2,2,12,9216]{3,2,1,0:T(8,128)} %reshape.97, f32[2,12,9216]{2,0,1:T(2,128)S(1)} %copy-done.1, f32[2,12,9216]{2,0,1:T(2,128)} %all-reduce.3.cloned.1.call-done), kind=kLoop, calls=%fused_computation.46 | loop fusion | flops 1327104 | bytes 5308416 | tf_op jit(solution)/shard_map/reduce_sum | solution.py:92
  463.7 268.7 %all-reduce.5.cloned.1.call-done = f32[2,12,9216]{2,0,1:T(2,128)} async-done(((f32[2,12,9216]{2,0,1:T(2,128)}), f32[2,12,9216]{2,0,1:T(2,128)}) %all-reduce.5.cloned.1.call-update) | async-done | bytes 884752 | tf_op jit(solution)/shard_map/psum | solution.py:93
  (85 shorter events, 72.7 us)
Async XLA Ops:
  7.2 2.1 copy-start.2
  7.2 270.5 %all-reduce.3.cloned.1.call-start = ((), (), s32[]{:S(2)}) async-start(), calls=%async_computation.2 | async-start | bytes 1769472 | tf_op jit(solution)/shard_map/psum | solution.py:13
  9.2 268.4 %copy-start = (f32[2,12,9216]{2,0,1:T(2,128)S(1)}, f32[2,12,9216]{2,0,1:T(2,128)}, u32[]{:S(2)}) copy-start(f32[2,12,9216]{2,0,1:T(2,128)} %param.5) | copy-start | bytes 2654212
  9.2 723.1 %all-reduce.5.cloned.1.call-start = ((), (), s32[]{:S(2)}) async-start(), calls=%async_computation.3 | async-start | bytes 1769472 | tf_op jit(solution)/shard_map/psum | solution.py:93
  319.9 10.5 %all-to-all-start.1 = ((f32[1,1,96,1152]{3,1,0,2:T(1,128)}), f32[1,1,96,1152]{3,1,0,2:T(1,128)S(1)}, u32[]{:S(2)}, u32[]{:S(2)}) async-start(f32[1,1,96,1152]{3,1,0,2:T(1,128)} %copy.57), calls=%async_computation.1 | async-start | bytes 884736 | tf_op jit(solution)/shard_map/while/body/eval_jaxpr/all_to_all | solution.py:85
  354.9 10.5 %all-to-all-start.1 = ((f32[1,1,96,1152]{3,1,0,2:T(1,128)}), f32[1,1,96,1152]{3,1,0,2:T(1,128)S(1)}, u32[]{:S(2)}, u32[]{:S(2)}) async-start(f32[1,1,96,1152]{3,1,0,2:T(1,128)} %copy.57), calls=%async_computation.1 | async-start | bytes 884736 | tf_op jit(solution)/shard_map/while/body/eval_jaxpr/all_to_all | solution.py:85
  389.8 10.5 %all-to-all-start.1 = ((f32[1,1,96,1152]{3,1,0,2:T(1,128)}), f32[1,1,96,1152]{3,1,0,2:T(1,128)S(1)}, u32[]{:S(2)}, u32[]{:S(2)}) async-start(f32[1,1,96,1152]{3,1,0,2:T(1,128)} %copy.57), calls=%async_computation.1 | async-start | bytes 884736 | tf_op jit(solution)/shard_map/while/body/eval_jaxpr/all_to_all | solution.py:85
  424.7 10.5 %all-to-all-start.1 = ((f32[1,1,96,1152]{3,1,0,2:T(1,128)}), f32[1,1,96,1152]{3,1,0,2:T(1,128)S(1)}, u32[]{:S(2)}, u32[]{:S(2)}) async-start(f32[1,1,96,1152]{3,1,0,2:T(1,128)} %copy.57), calls=%async_computation.1 | async-start | bytes 884736 | tf_op jit(solution)/shard_map/while/body/eval_jaxpr/all_to_all | solution.py:85
  450.1 2.5 copy-start.1
Sparse Core Ops, SparseCore 0:
  11.2 266.4 all-reduce.2
  462.4 269.8 all-reduce.4
